TPU v7x, 32 devices: a whole 2x2x4 slice. The times are simulated.
32 devices in a mesh: dp: 4 (over y, x), proto: 4 (over z), pair: 2 (over core).
Axes of the slice: x: 2, y: 2, z: 4, core: 2. Of those that a mesh axis runs over, the one named last changes fastest.
Arguments:
- student_patches: bfloat16 [2, 4096, 256], P('pair', 'dp'), may hold values from -2 to 2
- teacher_patches: bfloat16 [2, 4096, 256], P('pair', 'dp'), may hold values from -8 to 8
- student_proto: bfloat16 [65536, 256], P('proto'), may hold values from -4 to 4
- teacher_proto: bfloat16 [65536, 256], P('proto'), may hold values from -4 to 4
- masked_rows: int32 [2, 1024], P('pair', 'dp'), may hold values from 0 to 1023, as said below
Outputs:
- student_grad: float32 [2, 1024, 256], P('pair', 'dp')
Inputs may be any that keep to these rules, and one draw needn't show every extreme that they name: `masked_rows`: entries of one device's block name distinct patch rows of that device's 4 images (image g owns rows g * 256 to (g + 1) * 256 - 1); every image has between 16 and 112 masked patches.
All inputs are finite; a program needn't handle non-finite values.
Results may differ from a plain program's by a relative error of at most 0.00075.
The roundings to bfloat16 on the way count: a program that leaves them out, or rounds other values in their place, can miss the bound.
Values sent between devices are 32-bit elements; how exact they have to be, the bound alone decides.
No kernel may reach another device: no remote copies, remote signals or barrier semaphores. Data moves between devices by JAX's collectives and lax.ppermute only.
A program may use at most 128 MiB of HBM per device.

v0:
```python
import jax
import jax.numpy as jnp
from jax import lax
from jax.sharding import PartitionSpec as P

PATCHES = 256
ITERS = 2


teacher_temp = 0.07
student_temp = 0.1
epsilon = 1e-06


def inverse_norms(matrix):
    return lax.rsqrt(jnp.sum(jnp.square(matrix.astype(jnp.float32)), axis=-1) + epsilon)


def scores_of(features, protos):
    return lax.dot_general(
        features, protos, (((1,), (1,)), ((), ())), preferred_element_type=jnp.float32
    )


def on_device(student_patches, teacher_patches, student_proto, teacher_proto, masked_rows):
    slot_rows = masked_rows[0]
    count_slots = slot_rows.shape[0]
    images = student_patches.shape[1] // PATCHES
    image_of = slot_rows // PATCHES
    member = (image_of[:, None] == jnp.arange(images, dtype=jnp.int32)[None, :]).astype(jnp.float32)
    per_image = jnp.sum(member, axis=0)
    slot_count = jnp.sum(member * per_image[None, :], axis=1)
    weights = count_slots / images / slot_count
    student_rows = jnp.take(student_patches[0], slot_rows, axis=0)
    teacher_rows = jnp.take(teacher_patches[0], slot_rows, axis=0)
    teacher_scale = inverse_norms(teacher_proto)
    student_scale = inverse_norms(student_proto)
    teacher_inv = inverse_norms(teacher_rows)
    teacher_exp = jnp.exp(
        scores_of(teacher_rows, teacher_proto)
        * teacher_inv[:, None]
        * teacher_scale[None, :]
        / teacher_temp
    )
    row_factor = jnp.ones((count_slots,), jnp.float32)
    column_factor = jnp.ones((teacher_proto.shape[0],), jnp.float32)
    for sweep in range(ITERS):
        column_part = jnp.dot(row_factor, teacher_exp, precision=lax.Precision.HIGHEST)
        column_factor = 1.0 / lax.psum(column_part, ("dp", "pair"))
        row_part = jnp.dot(teacher_exp, column_factor, precision=lax.Precision.HIGHEST)
        row_factor = 1.0 / lax.psum(row_part, "proto")
    targets = (teacher_exp * row_factor[:, None] * (column_factor * student_scale)[None, :]).astype(
        jnp.bfloat16
    )
    student_inv = inverse_norms(student_rows)
    student_exp = jnp.exp(
        scores_of(student_rows, student_proto)
        * student_inv[:, None]
        * student_scale[None, :]
        / student_temp
    )
    partition_part = jnp.sum(student_exp, axis=1)
    partition = lax.psum(partition_part, "proto")
    pushed_w = (student_exp * student_scale[None, :]).astype(jnp.bfloat16)
    pushed = jnp.dot(pushed_w, student_proto, preferred_element_type=jnp.float32)
    pulled = jnp.dot(targets, student_proto, preferred_element_type=jnp.float32)
    pushed, pulled = lax.psum((pushed, pulled), "proto")
    inner_grad = (pushed / partition[:, None] - pulled) / student_temp
    rows_float = student_rows.astype(jnp.float32)
    row_dot = jnp.sum(rows_float * inner_grad, axis=1)
    cube = student_inv * student_inv * student_inv
    result_grad = weights[:, None] * (
        student_inv[:, None] * inner_grad - rows_float * (cube * row_dot)[:, None]
    )
    return result_grad[None]


def solution(mesh):
    placed = (
        P("pair", "dp", None),
        P("pair", "dp", None),
        P("proto", None),
        P("proto", None),
        P("pair", "dp"),
    )
    return jax.shard_map(
        on_device, mesh=mesh, in_specs=placed, out_specs=P("pair", "dp", None), check_vma=False
    )
```

profile of v0, /device:TPU:0, one launch (start us, length us, event | category | flops | bytes accessed | tf_op | source)
XLA Modules:
  0.0 296.8 jit_solution(648709590151249231)
XLA Ops:
  6.5 0.0 copy-start
  6.5 0.0 all-reduce.6.cloned.1.call-start
  6.5 0.7 compare_and_fusion
  7.3 0.7 and_select_fusion
  8.0 5.2 %multiply_reduce_fusion = f32[16384]{0:T(1024)S(1)} fusion(bf16[16384,256]{1,0:T(8,128)(2,1)} %param.10), kind=kLoop, calls=%fused_computation.11 | loop fusion | flops 12566528 | bytes 8454144 | tf_op jit(solution)/shard_map/reduce_sum | solution.py:16
  13.2 0.0 copy-done
  13.2 1.2 gather_fusion
  14.4 2.1 gather_fusion.1
  16.5 0.2 fusion.11
  16.7 12.4 %fusion.2 = f32[256,16384]{1,0:T(8,128)} fusion(bf16[16384,256]{1,0:T(8,128)(2,1)} %param.10, f32[16384]{0:T(1024)S(1)} %add_rsqrt_fusion, f32[256]{0:T(256)S(1)} %add_rsqrt_fusion.2, bf16[256,256]{1,0:T(8,128)(2,1)S(1)} %gather_fusion.1, pred[256]{0:T(512)(128)(4,1)S(1)} %compare_and_fusion), kind=kOutput, calls=%fused_computation.5 | convolution fusion | flops 2160132096 | bytes 25363712 | tf_op jit(solution)/shard_map/dot_general | solution.py:20
  29.1 12.1 %fusion.17 = f32[1,16384]{1,0:T(1,128)} fusion(f32[256,16384]{1,0:T(8,128)} %fusion.2), kind=kOutput, calls=%fused_computation.49 | convolution fusion | flops 50331648 | bytes 16842752 | tf_op jit(solution)/shard_map/dot_general | solution.py:48
  41.1 0.0 all-reduce.6.cloned.1.call-update
  41.2 0.2 all-reduce.8.cloned.1.call-start
  41.4 5.2 %multiply_reduce_fusion.1 = f32[16384]{0:T(1024)S(1)} fusion(bf16[16384,256]{1,0:T(8,128)(2,1)} %param.9), kind=kLoop, calls=%fused_computation.13 | loop fusion | flops 12566528 | bytes 8454144 | tf_op jit(solution)/shard_map/reduce_sum | solution.py:16
  46.6 50.6 %all-reduce.6.cloned.1.call-done = f32[16384]{0:T(1024)} async-done(((f32[16384]{0:T(1024)}), f32[16384]{0:T(1024)}) %all-reduce.6.cloned.1.call-update) | async-done | bytes 65552 | tf_op jit(solution)/shard_map/psum | solution.py:49
  97.2 0.9 broadcast_divide_fusion.1
  98.1 16.1 %fusion.23 = f32[1,256]{1,0:T(1,128)S(1)} fusion(f32[256,16384]{1,0:T(8,128)} %fusion.2, f32[16384,1]{0,1:T(1,128)S(1)} %bitcast.28), kind=kOutput, calls=%fused_computation.59 | convolution fusion | flops 50331648 | bytes 16843776 | tf_op jit(solution)/shard_map/dot_general | solution.py:50
  114.1 11.7 %psum.52 = f32[256]{0:T(256)S(1)} all-reduce(f32[256]{0:T(256)S(1)} %bitcast.30), channel_id=1, replica_groups=mesh['dp'=4,'proto'=4,'pair'=2] {'proto'}, use_global_device_ids=true, to_apply=%region_10.12 | all-reduce | flops 256 | bytes 2048 | tf_op jit(solution)/shard_map/psum | solution.py:51
  125.8 12.1 %fusion.24 = f32[1,16384]{1,0:T(1,128)} fusion(f32[256,1]{0,1:T(1,128)S(1)} %bitcast.31, f32[256,16384]{1,0:T(8,128)} %fusion.2), kind=kOutput, calls=%fused_computation.60 | convolution fusion | flops 50331648 | bytes 16843776 | tf_op jit(solution)/shard_map/dot_general | solution.py:48
  137.9 0.0 all-reduce.8.cloned.1.call-update
  137.9 0.3 all-reduce.10.cloned.1.call-start
  138.2 49.7 %all-reduce.8.cloned.1.call-done = f32[16384]{0:T(1024)} async-done(((f32[16384]{0:T(1024)}), f32[16384]{0:T(1024)}) %all-reduce.8.cloned.1.call-update) | async-done | bytes 65552 | tf_op jit(solution)/shard_map/psum | solution.py:49
  187.9 0.9 add_rsqrt_fusion.1
  188.8 16.1 %fusion.25 = f32[1,256]{1,0:T(1,128)S(1)} fusion(f32[256,16384]{1,0:T(8,128)} %fusion.2, f32[16384,1]{0,1:T(1,128)S(1)} %bitcast.25), kind=kOutput, calls=%fused_computation.61 | convolution fusion | flops 50331648 | bytes 16843776 | tf_op jit(solution)/shard_map/dot_general | solution.py:50
  204.8 12.6 %fusion.22 = (f32[256]{0:T(256)S(1)}, f32[256,16384]{1,0:T(8,128)}) fusion(f32[16384]{0:T(1024)S(1)} %get-tuple-element.12, f32[256]{0:T(256)S(1)} %add_rsqrt_fusion.3, bf16[16384,256]{1,0:T(8,128)(2,1)} %param.9, bf16[256,256]{1,0:T(8,128)(2,1)S(1)} %gather_fusion, pred[256]{0:T(512)(128)(4,1)S(1)} %compare_and_fusion), kind=kOutput, calls=%fused_computation.58 | convolution fusion | flops 2164326144 | bytes 25364736 | tf_op jit(solution)/shard_map/dot_general | solution.py:20
  217.5 11.7 %all-reduce = (f32[256]{0:T(256)S(1)}, f32[256]{0:T(256)S(1)}) all-reduce(f32[256]{0:T(256)S(1)} %bitcast.29, f32[256]{0:T(256)S(1)} %get-tuple-element.19), channel_id=1, replica_groups=mesh['dp'=4,'proto'=4,'pair'=2] {'proto'}, use_global_device_ids=true, to_apply=%region_12.14 | all-reduce | flops 512 | bytes 4096 | tf_op jit(solution)/shard_map/psum | solution.py:51
  229.1 11.2 %fusion.6 = f32[256,256]{1,0:T(8,128)} fusion(bf16[16384,256]{1,0:T(8,128)(2,1)} %param.9, f32[256,16384]{1,0:T(8,128)} %get-tuple-element.20, f32[16384]{0:T(1024)S(1)} %get-tuple-element.12), kind=kOutput, calls=%fused_computation.14 | convolution fusion | flops 2155872256 | bytes 25493504 | tf_op jit(solution)/shard_map/dot_general | solution.py:65
  240.3 11.2 %fusion.7 = f32[256,256]{1,0:T(8,128)} fusion(bf16[16384,256]{1,0:T(8,128)(2,1)} %param.9, f32[256,16384]{1,0:T(8,128)} %fusion.2, f32[16384]{0:T(1024)S(1)} %get-tuple-element.13, f32[256]{0:T(256)S(1)} %broadcast_divide_fusion.3), kind=kOutput, calls=%fused_computation.15 | convolution fusion | flops 2160066560 | bytes 25494528 | tf_op jit(solution)/shard_map/dot_general | solution.py:66
  251.6 0.0 all-reduce.10.cloned.1.call-update
  251.6 0.1 convert_reduce_fusion
  251.7 0.1 select_reduce_fusion
  251.8 35.3 %all-reduce.10.cloned.1.call-done = (f32[256,256]{1,0:T(8,128)}, f32[256,256]{1,0:T(8,128)}) async-done(((f32[256,256]{1,0:T(8,128)}, f32[256,256]{1,0:T(8,128)}), (f32[256,256]{1,0:T(8,128)}, f32[256,256]{1,0:T(8,128)})) %all-reduce.10.cloned.1.call-update) | async-done | bytes 524304 | tf_op jit(solution)/shard_map/psum | solution.py:67
  287.1 1.2 fusion.12
  288.3 2.0 fusion.15
  (8 shorter events, 0.1 us)
Async XLA Ops:
  6.5 6.7 %copy-start = (bf16[1,1024,256]{2,1,0:T(8,128)(2,1)S(1)}, bf16[1,1024,256]{2,1,0:T(8,128)(2,1)}, u32[]{:S(2)}) copy-start(bf16[1,1024,256]{2,1,0:T(8,128)(2,1)} %param.7) | copy-start | bytes 1572868
  6.5 90.7 %all-reduce.6.cloned.1.call-start = ((), (), s32[]{:S(2)}) async-start(), calls=%async_computation | async-start | bytes 131072 | tf_op jit(solution)/shard_map/psum | solution.py:49
  41.2 146.7 %all-reduce.8.cloned.1.call-start = ((), (), s32[]{:S(2)}) async-start(), calls=%async_computation.1 | async-start | bytes 131072 | tf_op jit(solution)/shard_map/psum | solution.py:49
  137.9 149.2 %all-reduce.10.cloned.1.call-start = ((), (), s32[]{:S(2)}) async-start(), calls=%async_computation.2 | async-start | bytes 1048576 | tf_op jit(solution)/shard_map/psum | solution.py:67
Sparse Core Ops, SparseCore 0:
  41.3 55.8 all-reduce.5
  138.0 49.8 all-reduce.7
  251.7 35.3 all-reduce.9
where the time goes:
time: 297 us
  waiting for transfers between devices  136 us (46%)
  matrix products  104 us (35%)
  blocking collectives  23.3 us (8%)
  other arithmetic  17.3 us (6%)
  between operations  13.2 us (4%)
  local copies, waits for them, and re-layouts  3.23 us (1%)
    psum x2, waiting for transfers between devices, on_device(): column_factor = 1.0 / lax.psum(column_part, ('dp', 'pair'))  100 us
    psum x1, waiting for transfers between devices, on_device(): pushed, pulled = lax.psum((pushed, pulled), 'proto')  35.3 us
    dot_general x2, matrix products, on_device(): jnp.dot(teacher_exp, column_factor, precision=lax.Precision.HIGHEST)  32.1 us
    dot_general x2, matrix products, scores_of(): lax.dot_general(features, protos, (((1,), (1,)), ((), ())), preferred_ele...  25 us
    dot_general x2, matrix products, on_device(): jnp.dot(row_factor, teacher_exp, precision=lax.Precision.HIGHEST)  24.1 us
    psum x2, blocking collectives, on_device(): row_factor = 1.0 / lax.psum(row_part, 'proto')  23.3 us
    dot_general x1, matrix products, on_device(): pulled = jnp.dot(targets, student_proto, preferred_element_type=jnp.float32)  11.2 us
    dot_general x1, matrix products, on_device(): jnp.dot(pushed_w, student_proto, preferred_element_type=jnp.float32)  11.2 us
  transfers between devices with their start and end apart: 3, of which 3 were waited for; matrix products, arithmetic and copies ran while one was open for 2% of the time, Pallas kernels for 0%

commit v1 on v0

v1 whole, which is shorter than its diff:
```python
import functools

import jax
import jax.numpy as jnp
from jax import lax
from jax.experimental import pallas as pl
from jax.experimental.pallas import tpu as pltpu
from jax.sharding import PartitionSpec as P

PATCHES = 256
LANES = 128
TILE = 256

teacher_temp = 0.07
student_temp = 0.1
epsilon = 1e-06
log2e = 1.4426950408889634

NT = (((1,), (1,)), ((), ()))
F32 = jnp.float32
BF16 = jnp.bfloat16
VMEM = pltpu.VMEM


def eye(n):
    return lax.broadcasted_iota(jnp.int32, (n, n), 0) == lax.broadcasted_iota(jnp.int32, (n, n), 1)


def to_column(row):
    n = row.shape[1]
    return jnp.sum(jnp.where(eye(n), jnp.broadcast_to(row, (n, n)), 0.0), axis=1, keepdims=True)


def to_row(column):
    n = column.shape[0]
    return jnp.sum(jnp.where(eye(n), jnp.broadcast_to(column, (n, n)), 0.0), axis=0, keepdims=True)


def tree(refs):
    parts = [ref[...] for ref in refs]
    while len(parts) > 1:
        parts = [parts[i] + parts[i + 1] for i in range(0, len(parts), 2)]
    return parts[0]


def gather_rows(slots, patches):
    column = to_column(slots.astype(F32)).astype(jnp.int32)
    count = slots.shape[1]
    rows = patches.shape[0]
    onehot = lax.broadcasted_iota(jnp.int32, (count, rows), 1) == column
    onehot = jnp.where(onehot, 1.0, 0.0).astype(BF16)
    return jnp.dot(onehot, patches, preferred_element_type=F32).astype(BF16)


def row_inverse(rows):
    wide = rows.astype(F32)
    return lax.rsqrt(jnp.sum(wide * wide, axis=1, keepdims=True) + epsilon)


def tile_scale(protos):
    gram = lax.dot_general(protos, protos, NT, preferred_element_type=F32)
    mask = eye(LANES)
    parts = []
    for k in range(0, TILE, LANES):
        parts.append(jnp.sum(jnp.where(mask, gram[k : k + LANES, k : k + LANES], 0.0), axis=0, keepdims=True))
    return lax.rsqrt(jnp.concatenate(parts, axis=1) + epsilon)


def teacher_kernel(slots_ref, patches_ref, protos_ref, exp_ref, sums_ref, rows_ref, factor_ref):
    block = protos_ref.shape[0]
    step = pl.program_id(0)

    @pl.when(step == 0)
    def _():
        rows = gather_rows(slots_ref[...], patches_ref[...])
        rows_ref[...] = rows
        factor = row_inverse(rows) * (log2e / teacher_temp)
        factor_ref[...] = jnp.broadcast_to(factor, factor_ref.shape)

    rows = rows_ref[...]
    for t in range(block // TILE):
        protos = protos_ref[t * TILE : (t + 1) * TILE, :]
        scores = lax.dot_general(rows, protos, NT, preferred_element_type=F32)
        scale = tile_scale(protos)
        for h in range(TILE // LANES):
            lanes = slice(h * LANES, (h + 1) * LANES)
            value = jnp.exp2(scores[:, lanes] * factor_ref[...] * scale[:, lanes])
            exp_ref[:, pl.ds(pl.multiple_of(step * block + t * TILE + h * LANES, LANES), LANES)] = value
            sums_ref[pl.ds(t * (TILE // LANES) + h, 1), :] = jnp.sum(value, axis=0, keepdims=True)


def student_kernel(
    slots_ref, patches_ref, protos_ref, scale_ref, part_ref, pushed_ref, rows_out_ref, rows_ref, factor_ref, total_ref, w_ref
):
    block = protos_ref.shape[0]
    step = pl.program_id(0)

    @pl.when(step == 0)
    def _():
        rows = gather_rows(slots_ref[...], patches_ref[...])
        rows_ref[...] = rows
        rows_out_ref[...] = rows
        factor = row_inverse(rows) * (log2e / student_temp)
        factor_ref[...] = jnp.broadcast_to(factor, factor_ref.shape)
        total_ref[...] = jnp.zeros_like(total_ref)
        pushed_ref[...] = jnp.zeros_like(pushed_ref)

    rows = rows_ref[...]
    for t in range(block // TILE):
        protos = protos_ref[t * TILE : (t + 1) * TILE, :]
        scores = lax.dot_general(rows, protos, NT, preferred_element_type=F32)
        scale = tile_scale(protos)
        for h in range(TILE // LANES):
            lanes = slice(h * LANES, (h + 1) * LANES)
            value = jnp.exp2(scores[:, lanes] * factor_ref[...] * scale[:, lanes])
            total_ref[...] += value
            w_ref[:, t * TILE + h * LANES : t * TILE + (h + 1) * LANES] = (value * scale[:, lanes]).astype(BF16)
            scale_ref[pl.ds(t * (TILE // LANES) + h, 1), :] = scale[:, lanes]
    pushed_ref[...] += jnp.dot(w_ref[...], protos_ref[...], preferred_element_type=F32)

    @pl.when(step == pl.num_programs(0) - 1)
    def _():
        part_ref[...] = to_row(jnp.sum(total_ref[...], axis=1, keepdims=True))


def row_pass_kernel(count, *refs):
    exp_ref = refs[0]
    column_ref, out_ref, total_ref = refs[1 + count :]
    column_ref[...] = 1.0 / tree(refs[1 : 1 + count])
    total_ref[...] = jnp.zeros_like(total_ref)
    chunks = exp_ref.shape[1] // LANES
    group = 8

    def body(g, carry):
        acc = total_ref[...]
        for k in range(group):
            c = g * group + k
            lanes = pl.ds(pl.multiple_of(c * LANES, LANES), LANES)
            acc = acc + exp_ref[:, lanes] * column_ref[pl.ds(c, 1), :]
        total_ref[...] = acc
        return carry

    lax.fori_loop(0, chunks // group, body, 0)
    out_ref[...] = to_row(jnp.sum(total_ref[...], axis=1, keepdims=True))


def column_pass_kernel(count, *refs):
    exp_ref = refs[0]
    out_ref, factor_ref = refs[1 + count :]
    factor = to_column(1.0 / tree(refs[1 : 1 + count]))
    factor_ref[...] = jnp.broadcast_to(factor, factor_ref.shape)
    chunks = exp_ref.shape[1] // LANES
    group = 4

    def body(g, carry):
        for k in range(group):
            c = g * group + k
            lanes = pl.ds(pl.multiple_of(c * LANES, LANES), LANES)
            out_ref[pl.ds(c, 1), :] = jnp.sum(exp_ref[:, lanes] * factor_ref[...], axis=0, keepdims=True)
        return carry

    lax.fori_loop(0, chunks // group, body, 0)


def pull_kernel(count, *refs):
    exp_ref = refs[0]
    column_ref, scale_ref, protos_ref, out_ref, factor_ref, w_ref = refs[1 + count :]
    block = protos_ref.shape[0]
    step = pl.program_id(0)

    @pl.when(step == 0)
    def _():
        factor = to_column(1.0 / tree(refs[1 : 1 + count]))
        factor_ref[...] = jnp.broadcast_to(factor, factor_ref.shape)
        out_ref[...] = jnp.zeros_like(out_ref)

    for k in range(block // LANES):
        lanes = pl.ds(pl.multiple_of(step * block + k * LANES, LANES), LANES)
        scale = column_ref[k : k + 1, :] * scale_ref[k : k + 1, :]
        w_ref[:, k * LANES : (k + 1) * LANES] = (exp_ref[:, lanes] * factor_ref[...] * scale).astype(BF16)
    out_ref[...] += jnp.dot(w_ref[...], protos_ref[...], preferred_element_type=F32)


def final_kernel(images, counts, *refs):
    out_ref = refs[-1]
    slots_ref, rows_ref = refs[:2]
    at = 2
    groups = []
    for count in counts:
        groups.append(tree(refs[at : at + count]))
        at += count
    partition, pushed, pulled = groups
    rows = rows_ref[...]
    inv = row_inverse(rows)
    wide = rows.astype(F32)
    grad = (pushed / to_column(partition) - pulled) / student_temp
    row_dot = jnp.sum(wide * grad, axis=1, keepdims=True)
    slots = slots_ref[...]
    total = slots.shape[1]
    image = (slots // PATCHES).astype(F32)
    same = to_column(image) == jnp.broadcast_to(image, (total, total))
    slot_count = jnp.sum(jnp.where(same, 1.0, 0.0), axis=1, keepdims=True)
    weights = total / images / slot_count
    out_ref[...] = weights * (inv * grad - wide * (inv * inv * inv * row_dot))


def exchange(value, axis):
    size = lax.axis_size(axis)
    if size > 4:
        while size > 4:
            size //= 2
            value = value + lax.ppermute(value, axis, [(i, i ^ size) for i in range(lax.axis_size(axis))])
    members = range(lax.axis_size(axis))
    return [value] + [lax.ppermute(value, axis, [(i, i ^ k) for i in members]) for k in range(1, size)]


def column_exchange(value):
    value = value + lax.ppermute(value, "pair", [(0, 1), (1, 0)])
    return exchange(value, "dp")


def call(kernel, name, out_shape, scratch=(), grid=None, in_specs=None, out_specs=None, limit=None):
    keep = {}
    if grid is not None:
        keep["grid"] = grid
    if in_specs is not None:
        keep["in_specs"] = in_specs
    if out_specs is not None:
        keep["out_specs"] = out_specs
    return pl.pallas_call(
        kernel,
        out_shape=out_shape,
        scratch_shapes=scratch,
        compiler_params=pltpu.CompilerParams(vmem_limit_bytes=limit or (36 << 20)),
        name=name,
        **keep,
    )


def whole(shape=None):
    return pl.BlockSpec(memory_space=VMEM)


def on_device(student_patches, teacher_patches, student_proto, teacher_proto, masked_rows):
    slots = masked_rows
    count = slots.shape[1]
    images = student_patches.shape[1] // PATCHES
    columns, width = teacher_proto.shape
    block = min(2048, columns)
    steps = columns // block
    chunks = columns // LANES
    shape = jax.ShapeDtypeStruct
    col_shape = shape((chunks, LANES), F32)
    row_shape = shape((1, count), F32)
    grad_shape = shape((count, width), F32)
    exp_shape = VMEM((count, columns), F32)
    col_block = pl.BlockSpec((block // LANES, LANES), lambda i: (i, 0))
    proto_block = pl.BlockSpec((block, width), lambda i: (i, 0))
    broad = VMEM((count, LANES), F32)
    full = whole()
    mib = 1 << 20

    exp, sums = call(
        teacher_kernel,
        "teacher",
        (exp_shape, col_shape),
        grid=(steps,),
        in_specs=[full, full, proto_block],
        out_specs=(full, col_block),
        scratch=[VMEM((count, width), BF16), broad],
    )(slots, teacher_patches[0], teacher_proto)

    scale, part, pushed, rows = call(
        student_kernel,
        "student",
        (col_shape, row_shape, grad_shape, shape((count, width), BF16)),
        grid=(steps,),
        in_specs=[full, full, proto_block],
        out_specs=(col_block, full, full, full),
        scratch=[VMEM((count, width), BF16), broad, broad, VMEM((count, block), BF16)],
    )(slots, student_patches[0], student_proto)

    def row_pass(parts):
        kernel = functools.partial(row_pass_kernel, len(parts))
        return call(kernel, "row_pass", (col_shape, row_shape), scratch=[broad])(exp, *parts)

    def column_pass(parts):
        kernel = functools.partial(column_pass_kernel, len(parts))
        return call(kernel, "column_pass", col_shape, scratch=[broad])(exp, *parts)

    column, row_part = row_pass(column_exchange(sums))
    sums = column_pass(exchange(row_part, "proto"))
    column, row_part = row_pass(column_exchange(sums))
    row_parts = exchange(row_part, "proto")
    pulled = call(
        functools.partial(pull_kernel, len(row_parts)),
        "pull",
        grad_shape,
        grid=(steps,),
        in_specs=[full] * (1 + len(row_parts)) + [col_block, col_block, proto_block],
        out_specs=full,
        scratch=[broad, VMEM((count, block), BF16)],
    )(exp, *row_parts, column, scale, student_proto)

    groups = [exchange(part, "proto"), exchange(pushed, "proto"), exchange(pulled, "proto")]
    flat = [value for group in groups for value in group]
    kernel = functools.partial(final_kernel, images, [len(group) for group in groups])
    return call(kernel, "final", grad_shape)(slots, rows, *flat)[None]


def solution(mesh):
    placed = (
        P("pair", "dp", None),
        P("pair", "dp", None),
        P("proto", None),
        P("proto", None),
        P("pair", "dp"),
    )
    return jax.shard_map(
        on_device, mesh=mesh, in_specs=placed, out_specs=P("pair", "dp", None), check_vma=False
    )
```

time: 297 us -> 125 us (0.42)
  matrix products: 104 us -> 0 us
  waiting for transfers between devices: 136 us -> 36.9 us
  Pallas kernels: 0 us -> 43.1 us
  starting transfers between devices: 0.49 us -> 29.5 us
  blocking collectives: 23.3 us -> 0 us
  other arithmetic: 17.3 us -> 0.02 us
  between operations: 13.2 us -> 0.11 us
  local copies, waits for them, and re-layouts: 3.23 us -> 13.6 us
    psum x3 -> x0, waiting for transfers between devices: 136 us -> none  [the longest x2 100 us: on_device(): column_factor = 1.0 / lax.psum(column_part, ('dp', 'pair'))]
    dot_general x8 -> x0, matrix products: 104 us -> none  [the longest x2 32.1 us: on_device(): jnp.dot(teacher_exp, column_factor, precision=lax.Precision.HIGHEST)]
    pallas_call x0 -> x7, Pallas kernels: none -> 43.1 us  [the longest x1 12.4 us: on_device(): call(student_kernel, 'student', (col_shape, row_shape, grad_shape, shape(...]
    ppermute x0 -> x23, waiting for transfers between devices: none -> 36.9 us  [the longest x21 35.7 us: exchange(): lax.ppermute(value, axis, [(i, i ^ k) for i in members])]
    ppermute x0 -> x23, starting transfers between devices: none -> 29.5 us  [the longest x21 29 us: exchange(): lax.ppermute(value, axis, [(i, i ^ k) for i in members])]
    psum x2 -> x0, blocking collectives: 23.3 us -> none  [on_device(): row_factor = 1.0 / lax.psum(row_part, 'proto')]
    unnamed x2 -> x14, local copies, waits for them, and re-layouts: 0.01 us -> 13.6 us
    reduce_sum x6 -> x0, other arithmetic: 12.1 us -> none  [the longest x3 10.7 us: inverse_norms(): jnp.sum(jnp.square(matrix.astype(jnp.float32)), axis=-1) + epsilon]
  transfers between devices with their start and end apart: 3 -> 23, of which waited for: 3 -> 12; matrix products, arithmetic and copies ran while one was open for 2% -> 0% of each run, Pallas kernels for 0% -> 26%
where the time goes in v1:
time: 125 us; the launch traced here: 123 us
  Pallas kernels  43.1 us (34%)
  waiting for transfers between devices  36.9 us (30%)
  starting transfers between devices  29.5 us (24%)
  local copies, waits for them, and re-layouts  13.6 us (11%)
    ppermute x21, waiting for transfers between devices, exchange(): lax.ppermute(value, axis, [(i, i ^ k) for i in members])  35.7 us
    ppermute x21, starting transfers between devices, exchange(): lax.ppermute(value, axis, [(i, i ^ k) for i in members])  29 us
    unnamed x14, local copies, waits for them, and re-layouts  13.6 us
    pallas_call x1, Pallas kernels, on_device(): call(student_kernel, 'student', (col_shape, row_shape, grad_shape, shape(...  12.4 us
    pallas_call x1, Pallas kernels, on_device(): call(functools.partial(pull_kernel, len(row_parts)), 'pull', grad_shape,...  10.9 us
    pallas_call x1, Pallas kernels, on_device(): call(teacher_kernel, 'teacher', (exp_shape, col_shape), grid=(steps,), in...  10.4 us
    pallas_call x2, Pallas kernels, row_pass(): call(kernel, 'row_pass', (col_shape, row_shape), scratch=[broad])  5.58 us
    pallas_call x1, Pallas kernels, column_pass(): return call(kernel, 'column_pass', col_shape, scratch=[broad])(exp, *parts)  2.84 us
  transfers between devices with their start and end apart: 23, of which 12 were waited for; matrix products, arithmetic and copies ran while one was open for 0% of the time, Pallas kernels for 26%

profile of v1, /device:TPU:0, one launch (start us, length us, event | category | flops | bytes accessed | tf_op | source)
XLA Modules:
  0.0 123.3 jit_solution(2480653344146125032)
XLA Ops:
  0.0 1.2 copy-done.3
  1.2 0.9 copy-done.5
  2.1 10.4 %teacher.1 = (f32[256,16384]{1,0:T(8,128)S(1)}, f32[128,128]{1,0:T(8,128)S(1)}) custom-call(s32[1,256]{1,0:T(1,128)S(1)} %copy-done.5, bf16[1024,256]{1,0:T(8,128)(2,1)S(1)} %bitcast.3, bf16[16384,256]{1,0:T(8,128)(2,1)} %protos_ref.3), custom_call_target="tpu_custom_call" | custom-call | tf_op jit(solution)/shard_map/teacher/pallas_call | solution.py:263
  12.5 5.7 %copy-done = f32[256,16384]{1,0:T(8,128)} copy-done((f32[256,16384]{1,0:T(8,128)}, f32[256,16384]{1,0:T(8,128)S(1)}, u32[]{:S(2)}) %copy-start) | copy-done | bytes 16777240
  18.2 0.5 collective-permute-start.6
  18.7 12.4 %student.1 = (f32[128,128]{1,0:T(8,128)S(1)}, f32[1,256]{1,0:T(1,128)S(1)}, f32[256,256]{1,0:T(8,128)S(1)}, bf16[256,256]{1,0:T(8,128)(2,1)S(1)}) custom-call(s32[1,256]{1,0:T(1,128)S(1)} %copy-done.5, bf16[1024,256]{1,0:T(8,128)(2,1)S(1)} %bitcast.4, bf16[16384,256]{1,0:T(8,128)(2,1)S(1)} %copy-done.2), custom_call_target="tpu_custom_call" | custom-call | tf_op jit(solution)/shard_map/student/pallas_call | solution.py:273
  31.1 2.6 %collective-permute-start.3 = (f32[256,256]{1,0:T(8,128)S(1)}, f32[256,256]{1,0:T(8,128)S(1)}, u32[]{:S(2)}, u32[]{:S(2)}) collective-permute-start(f32[256,256]{1,0:T(8,128)S(1)} %get-tuple-element.16.refs_6_), channel_id=1, source_target_pairs={{0,2},{2,0},{4,6},{6,4},{1,3},{3,1},{5,7},{7,5},{8,10},{10,8},{12,... | collective-permute-start | bytes 786440 | tf_op jit(solution)/shard_map/ppermute | solution.py:214
  33.7 0.0 collective-permute-done.6
  33.8 1.6 %collective-permute-start.7 = (f32[128,128]{1,0:T(8,128)S(1)}, f32[128,128]{1,0:T(8,128)S(1)}, u32[]{:S(2)}, u32[]{:S(2)}) collective-permute-start(f32[128,128]{1,0:T(8,128)S(1)} %add.6.refs_1_), channel_id=1, source_target_pairs={{0,8},{8,0},{16,24},{24,16},{1,9},{9,1},{17,25},{25,17},{2,10},{10... | collective-permute-start | bytes 196616 | tf_op jit(solution)/shard_map/ppermute | solution.py:214
  35.3 1.5 %collective-permute-start.8 = (f32[128,128]{1,0:T(8,128)S(1)}, f32[128,128]{1,0:T(8,128)S(1)}, u32[]{:S(2)}, u32[]{:S(2)}) collective-permute-start(f32[128,128]{1,0:T(8,128)S(1)} %add.6.refs_1_), channel_id=1, source_target_pairs={{0,16},{8,24},{16,0},{24,8},{1,17},{9,25},{17,1},{25,9},{2,18},{10... | collective-permute-start | bytes 196616 | tf_op jit(solution)/shard_map/ppermute | solution.py:214
  36.8 0.5 collective-permute-start.9
  37.3 0.8 collective-permute-done.7.refs_2_
  38.1 1.5 %collective-permute-done.8.refs_3_ = f32[128,128]{1,0:T(8,128)S(1)} collective-permute-done((f32[128,128]{1,0:T(8,128)S(1)}, f32[128,128]{1,0:T(8,128)S(1)}, u32[]{:S(2)}, u32[]{:S(2)}) %collective-permute-start.8) | collective-permute-done | bytes 65568 | tf_op jit(solution)/shard_map/ppermute | solution.py:214
  39.6 2.4 %collective-permute-done.9.refs_4_ = f32[128,128]{1,0:T(8,128)S(1)} collective-permute-done((f32[128,128]{1,0:T(8,128)S(1)}, f32[128,128]{1,0:T(8,128)S(1)}, u32[]{:S(2)}, u32[]{:S(2)}) %collective-permute-start.9) | collective-permute-done | bytes 65568 | tf_op jit(solution)/shard_map/ppermute | solution.py:214
  42.0 5.8 %copy-done.1 = f32[256,16384]{1,0:T(8,128)S(1)} copy-done((f32[256,16384]{1,0:T(8,128)S(1)}, f32[256,16384]{1,0:T(8,128)}, u32[]{:S(2)}) %copy-start.1) | copy-done | bytes 16777240
  47.8 3.0 %row_pass.2 = (f32[128,128]{1,0:T(8,128)}, f32[1,256]{1,0:T(1,128)S(1)}) custom-call(f32[256,16384]{1,0:T(8,128)S(1)} %copy-done.1, f32[128,128]{1,0:T(8,128)S(1)} %add.6.refs_1_, f32[128,128]{1,0:T(8,128)S(1)} %collective-permute-done.7.refs_2_, f32[128,128]{1,0:T(8,128)S(1)} %collective-permute-done.8.refs_3_, f32[128,128]{1,0:T(8,128)S(1)} %collective-permute-done.9.refs_4_), custom_call_target="tpu_custom_call" | custom-call | tf_op jit(solution)/shard_map/row_pass/pallas_call | solution.py:285
  50.8 0.5 collective-permute-start.10
  51.3 2.6 %collective-permute-start.11 = (f32[1,256]{1,0:T(1,128)S(1)}, f32[1,256]{1,0:T(1,128)S(1)}, u32[]{:S(2)}, u32[]{:S(2)}) collective-permute-start(f32[1,256]{1,0:T(1,128)S(1)} %get-tuple-element.19.refs_1_), channel_id=1, source_target_pairs={{0,4},{2,6},{4,0},{6,2},{1,5},{3,7},{5,1},{7,3},{8,12},{10,14},{12... | collective-permute-start | bytes 3080 | tf_op jit(solution)/shard_map/ppermute | solution.py:214
  53.8 1.3 %collective-permute-start.12 = (f32[1,256]{1,0:T(1,128)S(1)}, f32[1,256]{1,0:T(1,128)S(1)}, u32[]{:S(2)}, u32[]{:S(2)}) collective-permute-start(f32[1,256]{1,0:T(1,128)S(1)} %get-tuple-element.19.refs_1_), channel_id=1, source_target_pairs={{0,6},{2,4},{4,2},{6,0},{1,7},{3,5},{5,3},{7,1},{8,14},{10,12},{12... | collective-permute-start | bytes 3080 | tf_op jit(solution)/shard_map/ppermute | solution.py:214
  55.2 0.0 collective-permute-done.10.refs_2_
  55.2 0.5 collective-permute-done.11.refs_3_
  55.7 3.5 %collective-permute-done.12.refs_4_ = f32[1,256]{1,0:T(1,128)S(1)} collective-permute-done((f32[1,256]{1,0:T(1,128)S(1)}, f32[1,256]{1,0:T(1,128)S(1)}, u32[]{:S(2)}, u32[]{:S(2)}) %collective-permute-start.12) | collective-permute-done | bytes 1056 | tf_op jit(solution)/shard_map/ppermute | solution.py:214
  59.2 2.8 %column_pass.1 = f32[128,128]{1,0:T(8,128)S(1)} custom-call(f32[256,16384]{1,0:T(8,128)S(1)} %copy-done.1, f32[1,256]{1,0:T(1,128)S(1)} %get-tuple-element.19.refs_1_, f32[1,256]{1,0:T(1,128)S(1)} %collective-permute-done.10.refs_2_, f32[1,256]{1,0:T(1,128)S(1)} %collective-permute-done.11.refs_3_, f32[1,256]{1,0:T(1,128)S(1)} %collective-permute-done.12.refs_4_), custom_call_target="tpu_custom_call" | custom-call | tf_op jit(solution)/shard_map/column_pass/pallas_call | solution.py:289
  62.1 0.1 collective-permute-start.13
  62.1 1.2 %collective-permute-done.13 = f32[128,128]{1,0:T(8,128)S(1)} collective-permute-done((f32[128,128]{1,0:T(8,128)S(1)}, f32[128,128]{1,0:T(8,128)S(1)}, u32[]{:S(2)}, u32[]{:S(2)}) %collective-permute-start.13) | collective-permute-done | bytes 65568 | tf_op jit(solution)/shard_map/ppermute | solution.py:218
  63.4 0.6 collective-permute-start.14
  64.0 0.5 collective-permute-start.15
  64.5 2.4 %collective-permute-start.16 = (f32[128,128]{1,0:T(8,128)S(1)}, f32[128,128]{1,0:T(8,128)S(1)}, u32[]{:S(2)}, u32[]{:S(2)}) collective-permute-start(f32[128,128]{1,0:T(8,128)S(1)} %add.7.refs_1_), channel_id=1, source_target_pairs={{0,24},{8,16},{16,8},{24,0},{1,25},{9,17},{17,9},{25,1},{2,26},{10... | collective-permute-start | bytes 196616 | tf_op jit(solution)/shard_map/ppermute | solution.py:214
  67.0 0.8 collective-permute-done.14.refs_2_
  67.8 1.2 collective-permute-done.15.refs_3_
  69.0 0.7 collective-permute-done.16.refs_4_
  69.7 2.5 %row_pass.3 = (f32[128,128]{1,0:T(8,128)S(1)}, f32[1,256]{1,0:T(1,128)S(1)}) custom-call(f32[256,16384]{1,0:T(8,128)S(1)} %copy-done.1, f32[128,128]{1,0:T(8,128)S(1)} %add.7.refs_1_, f32[128,128]{1,0:T(8,128)S(1)} %collective-permute-done.14.refs_2_, f32[128,128]{1,0:T(8,128)S(1)} %collective-permute-done.15.refs_3_, ...), custom_call_target="tpu_custom_call" | custom-call | tf_op jit(solution)/shard_map/row_pass/pallas_call | solution.py:285
  72.2 0.1 collective-permute-start.17
  72.3 1.9 %collective-permute-start.18 = (f32[1,256]{1,0:T(1,128)S(1)}, f32[1,256]{1,0:T(1,128)S(1)}, u32[]{:S(2)}, u32[]{:S(2)}) collective-permute-start(f32[1,256]{1,0:T(1,128)S(1)} %get-tuple-element.20.refs_1_), channel_id=1, source_target_pairs={{0,4},{2,6},{4,0},{6,2},{1,5},{3,7},{5,1},{7,3},{8,12},{10,14},{12... | collective-permute-start | bytes 3080 | tf_op jit(solution)/shard_map/ppermute | solution.py:214
  74.2 2.5 %collective-permute-start.19 = (f32[1,256]{1,0:T(1,128)S(1)}, f32[1,256]{1,0:T(1,128)S(1)}, u32[]{:S(2)}, u32[]{:S(2)}) collective-permute-start(f32[1,256]{1,0:T(1,128)S(1)} %get-tuple-element.20.refs_1_), channel_id=1, source_target_pairs={{0,6},{2,4},{4,2},{6,0},{1,7},{3,5},{5,3},{7,1},{8,14},{10,12},{12... | collective-permute-start | bytes 3080 | tf_op jit(solution)/shard_map/ppermute | solution.py:214
  76.7 1.9 %collective-permute-start.1 = (f32[1,256]{1,0:T(1,128)S(1)}, f32[1,256]{1,0:T(1,128)S(1)}, u32[]{:S(2)}, u32[]{:S(2)}) collective-permute-start(f32[1,256]{1,0:T(1,128)S(1)} %get-tuple-element.15.refs_2_), channel_id=1, source_target_pairs={{0,4},{2,6},{4,0},{6,2},{1,5},{3,7},{5,1},{7,3},{8,12},{10,14},{12... | collective-permute-start | bytes 3080 | tf_op jit(solution)/shard_map/ppermute | solution.py:214
  78.6 2.5 %collective-permute-start.2 = (f32[1,256]{1,0:T(1,128)S(1)}, f32[1,256]{1,0:T(1,128)S(1)}, u32[]{:S(2)}, u32[]{:S(2)}) collective-permute-start(f32[1,256]{1,0:T(1,128)S(1)} %get-tuple-element.15.refs_2_), channel_id=1, source_target_pairs={{0,6},{2,4},{4,2},{6,0},{1,7},{3,5},{5,3},{7,1},{8,14},{10,12},{12... | collective-permute-start | bytes 3080 | tf_op jit(solution)/shard_map/ppermute | solution.py:214
  81.1 0.0 collective-permute-done.19.refs_4_
  81.1 0.0 collective-permute-start.4
  81.1 10.9 %pull.1.refs_10_ = f32[256,256]{1,0:T(8,128)S(1)} custom-call(f32[256,16384]{1,0:T(8,128)} %copy-done, f32[1,256]{1,0:T(1,128)S(1)} %get-tuple-element.20.refs_1_, f32[1,256]{1,0:T(1,128)S(1)} %collective-permute-done.17.refs_2_, f32[1,256]{1,0:T(1,128)S(1)} %collective-permute-done.18.refs_3_, f32[1,256]{1,0:T(1,128)S(1)} %collective-permute-done.19.refs_4_, ...), custom_call_target="tpu_custom_call" | custom-call | tf_op jit(solution)/shard_map/pull/pallas_call | solution.py:295
  92.0 1.5 %collective-permute-start.5 = (f32[256,256]{1,0:T(8,128)S(1)}, f32[256,256]{1,0:T(8,128)S(1)}, u32[]{:S(2)}, u32[]{:S(2)}) collective-permute-start(f32[256,256]{1,0:T(8,128)S(1)} %get-tuple-element.16.refs_6_), channel_id=1, source_target_pairs={{0,6},{2,4},{4,2},{6,0},{1,7},{3,5},{5,3},{7,1},{8,14},{10,12},{12... | collective-permute-start | bytes 786440 | tf_op jit(solution)/shard_map/ppermute | solution.py:214
  93.5 2.0 %collective-permute-start.20 = (f32[256,256]{1,0:T(8,128)S(1)}, f32[256,256]{1,0:T(8,128)S(1)}, u32[]{:S(2)}, u32[]{:S(2)}) collective-permute-start(f32[256,256]{1,0:T(8,128)S(1)} %pull.1.refs_10_), channel_id=1, source_target_pairs={{0,2},{2,0},{4,6},{6,4},{1,3},{3,1},{5,7},{7,5},{8,10},{10,8},{12,... | collective-permute-start | bytes 786440 | tf_op jit(solution)/shard_map/ppermute | solution.py:214
  95.5 0.9 collective-permute-start.21
  96.5 1.5 %collective-permute-start.22 = (f32[256,256]{1,0:T(8,128)S(1)}, f32[256,256]{1,0:T(8,128)S(1)}, u32[]{:S(2)}, u32[]{:S(2)}) collective-permute-start(f32[256,256]{1,0:T(8,128)S(1)} %pull.1.refs_10_), channel_id=1, source_target_pairs={{0,6},{2,4},{4,2},{6,0},{1,7},{3,5},{5,3},{7,1},{8,14},{10,12},{12... | collective-permute-start | bytes 786440 | tf_op jit(solution)/shard_map/ppermute | solution.py:214
  98.0 5.1 %collective-permute-done.5.refs_9_ = f32[256,256]{1,0:T(8,128)S(1)} collective-permute-done((f32[256,256]{1,0:T(8,128)S(1)}, f32[256,256]{1,0:T(8,128)S(1)}, u32[]{:S(2)}, u32[]{:S(2)}) %collective-permute-start.5) | collective-permute-done | bytes 262176 | tf_op jit(solution)/shard_map/ppermute | solution.py:214
  103.1 2.7 %collective-permute-done.20.refs_11_ = f32[256,256]{1,0:T(8,128)S(1)} collective-permute-done((f32[256,256]{1,0:T(8,128)S(1)}, f32[256,256]{1,0:T(8,128)S(1)}, u32[]{:S(2)}, u32[]{:S(2)}) %collective-permute-start.20) | collective-permute-done | bytes 262176 | tf_op jit(solution)/shard_map/ppermute | solution.py:214
  105.9 16.4 %collective-permute-done.21.refs_12_ = f32[256,256]{1,0:T(8,128)S(1)} collective-permute-done((f32[256,256]{1,0:T(8,128)S(1)}, f32[256,256]{1,0:T(8,128)S(1)}, u32[]{:S(2)}, u32[]{:S(2)}) %collective-permute-start.21) | collective-permute-done | bytes 262176 | tf_op jit(solution)/shard_map/ppermute | solution.py:214
  122.2 1.1 final.1
  (21 shorter events, 0.1 us)
Async XLA Ops:
  0.0 18.7 %copy-start.2 = (bf16[16384,256]{1,0:T(8,128)(2,1)S(1)}, bf16[16384,256]{1,0:T(8,128)(2,1)}, u32[]{:S(2)}) copy-start(bf16[16384,256]{1,0:T(8,128)(2,1)} %refs_7_.1) | copy-start | bytes 25165828
  0.0 1.2 copy-start.3
  1.2 0.9 copy-start.5
  2.1 16.6 %copy-start.4 = (bf16[1,1024,256]{2,1,0:T(8,128)(2,1)S(1)}, bf16[1,1024,256]{2,1,0:T(8,128)(2,1)}, u32[]{:S(2)}) copy-start(bf16[1,1024,256]{2,1,0:T(8,128)(2,1)} %param.5) | copy-start | bytes 1572868
  12.5 5.7 %copy-start = (f32[256,16384]{1,0:T(8,128)}, f32[256,16384]{1,0:T(8,128)S(1)}, u32[]{:S(2)}) copy-start(f32[256,16384]{1,0:T(8,128)S(1)} %get-tuple-element.17.refs_0_) | copy-start | bytes 50331652
  18.2 15.5 %collective-permute-start.6 = (f32[128,128]{1,0:T(8,128)S(1)}, f32[128,128]{1,0:T(8,128)S(1)}, u32[]{:S(2)}, u32[]{:S(2)}) collective-permute-start(f32[128,128]{1,0:T(8,128)S(1)} %get-tuple-element.18), channel_id=1, source_target_pairs={{0,1},{1,0},{2,3},{3,2},{4,5},{5,4},{6,7},{7,6},{8,9},{9,8},{10,11... | collective-permute-start | bytes 196616 | tf_op jit(solution)/shard_map/ppermute | solution.py:218
  31.1 65.4 %collective-permute-start.3 = (f32[256,256]{1,0:T(8,128)S(1)}, f32[256,256]{1,0:T(8,128)S(1)}, u32[]{:S(2)}, u32[]{:S(2)}) collective-permute-start(f32[256,256]{1,0:T(8,128)S(1)} %get-tuple-element.16.refs_6_), channel_id=1, source_target_pairs={{0,2},{2,0},{4,6},{6,4},{1,3},{3,1},{5,7},{7,5},{8,10},{10,8},{12,... | collective-permute-start | bytes 786440 | tf_op jit(solution)/shard_map/ppermute | solution.py:214
  33.8 4.3 %collective-permute-start.7 = (f32[128,128]{1,0:T(8,128)S(1)}, f32[128,128]{1,0:T(8,128)S(1)}, u32[]{:S(2)}, u32[]{:S(2)}) collective-permute-start(f32[128,128]{1,0:T(8,128)S(1)} %add.6.refs_1_), channel_id=1, source_target_pairs={{0,8},{8,0},{16,24},{24,16},{1,9},{9,1},{17,25},{25,17},{2,10},{10... | collective-permute-start | bytes 196616 | tf_op jit(solution)/shard_map/ppermute | solution.py:214
  35.3 4.3 %collective-permute-start.8 = (f32[128,128]{1,0:T(8,128)S(1)}, f32[128,128]{1,0:T(8,128)S(1)}, u32[]{:S(2)}, u32[]{:S(2)}) collective-permute-start(f32[128,128]{1,0:T(8,128)S(1)} %add.6.refs_1_), channel_id=1, source_target_pairs={{0,16},{8,24},{16,0},{24,8},{1,17},{9,25},{17,1},{25,9},{2,18},{10... | collective-permute-start | bytes 196616 | tf_op jit(solution)/shard_map/ppermute | solution.py:214
  36.8 5.2 %collective-permute-start.9 = (f32[128,128]{1,0:T(8,128)S(1)}, f32[128,128]{1,0:T(8,128)S(1)}, u32[]{:S(2)}, u32[]{:S(2)}) collective-permute-start(f32[128,128]{1,0:T(8,128)S(1)} %add.6.refs_1_), channel_id=1, source_target_pairs={{0,24},{8,16},{16,8},{24,0},{1,25},{9,17},{17,9},{25,1},{2,26},{10... | collective-permute-start | bytes 196616 | tf_op jit(solution)/shard_map/ppermute | solution.py:214
  42.0 5.8 %copy-start.1 = (f32[256,16384]{1,0:T(8,128)S(1)}, f32[256,16384]{1,0:T(8,128)}, u32[]{:S(2)}) copy-start(f32[256,16384]{1,0:T(8,128)} %copy-done) | copy-start | bytes 50331652
  50.8 4.4 %collective-permute-start.10 = (f32[1,256]{1,0:T(1,128)S(1)}, f32[1,256]{1,0:T(1,128)S(1)}, u32[]{:S(2)}, u32[]{:S(2)}) collective-permute-start(f32[1,256]{1,0:T(1,128)S(1)} %get-tuple-element.19.refs_1_), channel_id=1, source_target_pairs={{0,2},{2,0},{4,6},{6,4},{1,3},{3,1},{5,7},{7,5},{8,10},{10,8},{12,... | collective-permute-start | bytes 3080 | tf_op jit(solution)/shard_map/ppermute | solution.py:214
  51.3 4.5 %collective-permute-start.11 = (f32[1,256]{1,0:T(1,128)S(1)}, f32[1,256]{1,0:T(1,128)S(1)}, u32[]{:S(2)}, u32[]{:S(2)}) collective-permute-start(f32[1,256]{1,0:T(1,128)S(1)} %get-tuple-element.19.refs_1_), channel_id=1, source_target_pairs={{0,4},{2,6},{4,0},{6,2},{1,5},{3,7},{5,1},{7,3},{8,12},{10,14},{12... | collective-permute-start | bytes 3080 | tf_op jit(solution)/shard_map/ppermute | solution.py:214
  53.8 5.4 %collective-permute-start.12 = (f32[1,256]{1,0:T(1,128)S(1)}, f32[1,256]{1,0:T(1,128)S(1)}, u32[]{:S(2)}, u32[]{:S(2)}) collective-permute-start(f32[1,256]{1,0:T(1,128)S(1)} %get-tuple-element.19.refs_1_), channel_id=1, source_target_pairs={{0,6},{2,4},{4,2},{6,0},{1,7},{3,5},{5,3},{7,1},{8,14},{10,12},{12... | collective-permute-start | bytes 3080 | tf_op jit(solution)/shard_map/ppermute | solution.py:214
  62.1 1.3 %collective-permute-start.13 = (f32[128,128]{1,0:T(8,128)S(1)}, f32[128,128]{1,0:T(8,128)S(1)}, u32[]{:S(2)}, u32[]{:S(2)}) collective-permute-start(f32[128,128]{1,0:T(8,128)S(1)} %column_pass.1), channel_id=1, source_target_pairs={{0,1},{1,0},{2,3},{3,2},{4,5},{5,4},{6,7},{7,6},{8,9},{9,8},{10,11... | collective-permute-start | bytes 196616 | tf_op jit(solution)/shard_map/ppermute | solution.py:218
  63.4 4.4 %collective-permute-start.14 = (f32[128,128]{1,0:T(8,128)S(1)}, f32[128,128]{1,0:T(8,128)S(1)}, u32[]{:S(2)}, u32[]{:S(2)}) collective-permute-start(f32[128,128]{1,0:T(8,128)S(1)} %add.7.refs_1_), channel_id=1, source_target_pairs={{0,8},{8,0},{16,24},{24,16},{1,9},{9,1},{17,25},{25,17},{2,10},{10... | collective-permute-start | bytes 196616 | tf_op jit(solution)/shard_map/ppermute | solution.py:214
  64.0 5.0 %collective-permute-start.15 = (f32[128,128]{1,0:T(8,128)S(1)}, f32[128,128]{1,0:T(8,128)S(1)}, u32[]{:S(2)}, u32[]{:S(2)}) collective-permute-start(f32[128,128]{1,0:T(8,128)S(1)} %add.7.refs_1_), channel_id=1, source_target_pairs={{0,16},{8,24},{16,0},{24,8},{1,17},{9,25},{17,1},{25,9},{2,18},{10... | collective-permute-start | bytes 196616 | tf_op jit(solution)/shard_map/ppermute | solution.py:214
  64.5 5.2 %collective-permute-start.16 = (f32[128,128]{1,0:T(8,128)S(1)}, f32[128,128]{1,0:T(8,128)S(1)}, u32[]{:S(2)}, u32[]{:S(2)}) collective-permute-start(f32[128,128]{1,0:T(8,128)S(1)} %add.7.refs_1_), channel_id=1, source_target_pairs={{0,24},{8,16},{16,8},{24,0},{1,25},{9,17},{17,9},{25,1},{2,26},{10... | collective-permute-start | bytes 196616 | tf_op jit(solution)/shard_map/ppermute | solution.py:214
  72.2 4.5 %collective-permute-start.17 = (f32[1,256]{1,0:T(1,128)S(1)}, f32[1,256]{1,0:T(1,128)S(1)}, u32[]{:S(2)}, u32[]{:S(2)}) collective-permute-start(f32[1,256]{1,0:T(1,128)S(1)} %get-tuple-element.20.refs_1_), channel_id=1, source_target_pairs={{0,2},{2,0},{4,6},{6,4},{1,3},{3,1},{5,7},{7,5},{8,10},{10,8},{12,... | collective-permute-start | bytes 3080 | tf_op jit(solution)/shard_map/ppermute | solution.py:214
  72.3 6.3 %collective-permute-start.18 = (f32[1,256]{1,0:T(1,128)S(1)}, f32[1,256]{1,0:T(1,128)S(1)}, u32[]{:S(2)}, u32[]{:S(2)}) collective-permute-start(f32[1,256]{1,0:T(1,128)S(1)} %get-tuple-element.20.refs_1_), channel_id=1, source_target_pairs={{0,4},{2,6},{4,0},{6,2},{1,5},{3,7},{5,1},{7,3},{8,12},{10,14},{12... | collective-permute-start | bytes 3080 | tf_op jit(solution)/shard_map/ppermute | solution.py:214
  74.2 6.9 %collective-permute-start.19 = (f32[1,256]{1,0:T(1,128)S(1)}, f32[1,256]{1,0:T(1,128)S(1)}, u32[]{:S(2)}, u32[]{:S(2)}) collective-permute-start(f32[1,256]{1,0:T(1,128)S(1)} %get-tuple-element.20.refs_1_), channel_id=1, source_target_pairs={{0,6},{2,4},{4,2},{6,0},{1,7},{3,5},{5,3},{7,1},{8,14},{10,12},{12... | collective-permute-start | bytes 3080 | tf_op jit(solution)/shard_map/ppermute | solution.py:214
  76.7 15.3 %collective-permute-start = (f32[1,256]{1,0:T(1,128)S(1)}, f32[1,256]{1,0:T(1,128)S(1)}, u32[]{:S(2)}, u32[]{:S(2)}) collective-permute-start(f32[1,256]{1,0:T(1,128)S(1)} %get-tuple-element.15.refs_2_), channel_id=1, source_target_pairs={{0,2},{2,0},{4,6},{6,4},{1,3},{3,1},{5,7},{7,5},{8,10},{10,8},{12,... | collective-permute-start | bytes 3080 | tf_op jit(solution)/shard_map/ppermute | solution.py:214
  76.7 16.8 %collective-permute-start.1 = (f32[1,256]{1,0:T(1,128)S(1)}, f32[1,256]{1,0:T(1,128)S(1)}, u32[]{:S(2)}, u32[]{:S(2)}) collective-permute-start(f32[1,256]{1,0:T(1,128)S(1)} %get-tuple-element.15.refs_2_), channel_id=1, source_target_pairs={{0,4},{2,6},{4,0},{6,2},{1,5},{3,7},{5,1},{7,3},{8,12},{10,14},{12... | collective-permute-start | bytes 3080 | tf_op jit(solution)/shard_map/ppermute | solution.py:214
  78.6 17.0 %collective-permute-start.2 = (f32[1,256]{1,0:T(1,128)S(1)}, f32[1,256]{1,0:T(1,128)S(1)}, u32[]{:S(2)}, u32[]{:S(2)}) collective-permute-start(f32[1,256]{1,0:T(1,128)S(1)} %get-tuple-element.15.refs_2_), channel_id=1, source_target_pairs={{0,6},{2,4},{4,2},{6,0},{1,7},{3,5},{5,3},{7,1},{8,14},{10,12},{12... | collective-permute-start | bytes 3080 | tf_op jit(solution)/shard_map/ppermute | solution.py:214
  81.1 16.9 %collective-permute-start.4 = (f32[256,256]{1,0:T(8,128)S(1)}, f32[256,256]{1,0:T(8,128)S(1)}, u32[]{:S(2)}, u32[]{:S(2)}) collective-permute-start(f32[256,256]{1,0:T(8,128)S(1)} %get-tuple-element.16.refs_6_), channel_id=1, source_target_pairs={{0,4},{2,6},{4,0},{6,2},{1,5},{3,7},{5,1},{7,3},{8,12},{10,14},{12... | collective-permute-start | bytes 786440 | tf_op jit(solution)/shard_map/ppermute | solution.py:214
  81.1 41.2 %copy-start.6 = (s32[1,256]{1,0:T(1,128)S(1)}, s32[1,256]{1,0:T(1,128)}, u32[]{:S(2)}) copy-start(s32[1,256]{1,0:T(1,128)} %refs_0_.1) | copy-start | bytes 3076
  92.0 11.1 %collective-permute-start.5 = (f32[256,256]{1,0:T(8,128)S(1)}, f32[256,256]{1,0:T(8,128)S(1)}, u32[]{:S(2)}, u32[]{:S(2)}) collective-permute-start(f32[256,256]{1,0:T(8,128)S(1)} %get-tuple-element.16.refs_6_), channel_id=1, source_target_pairs={{0,6},{2,4},{4,2},{6,0},{1,7},{3,5},{5,3},{7,1},{8,14},{10,12},{12... | collective-permute-start | bytes 786440 | tf_op jit(solution)/shard_map/ppermute | solution.py:214
  93.5 12.4 %collective-permute-start.20 = (f32[256,256]{1,0:T(8,128)S(1)}, f32[256,256]{1,0:T(8,128)S(1)}, u32[]{:S(2)}, u32[]{:S(2)}) collective-permute-start(f32[256,256]{1,0:T(8,128)S(1)} %pull.1.refs_10_), channel_id=1, source_target_pairs={{0,2},{2,0},{4,6},{6,4},{1,3},{3,1},{5,7},{7,5},{8,10},{10,8},{12,... | collective-permute-start | bytes 786440 | tf_op jit(solution)/shard_map/ppermute | solution.py:214
  95.5 26.7 %collective-permute-start.21 = (f32[256,256]{1,0:T(8,128)S(1)}, f32[256,256]{1,0:T(8,128)S(1)}, u32[]{:S(2)}, u32[]{:S(2)}) collective-permute-start(f32[256,256]{1,0:T(8,128)S(1)} %pull.1.refs_10_), channel_id=1, source_target_pairs={{0,4},{2,6},{4,0},{6,2},{1,5},{3,7},{5,1},{7,3},{8,12},{10,14},{12... | collective-permute-start | bytes 786440 | tf_op jit(solution)/shard_map/ppermute | solution.py:214
  96.5 25.8 %collective-permute-start.22 = (f32[256,256]{1,0:T(8,128)S(1)}, f32[256,256]{1,0:T(8,128)S(1)}, u32[]{:S(2)}, u32[]{:S(2)}) collective-permute-start(f32[256,256]{1,0:T(8,128)S(1)} %pull.1.refs_10_), channel_id=1, source_target_pairs={{0,6},{2,4},{4,2},{6,0},{1,7},{3,5},{5,3},{7,1},{8,14},{10,12},{12... | collective-permute-start | bytes 786440 | tf_op jit(solution)/shard_map/ppermute | solution.py:214
